TPU v7x, 32 devices: a whole 2x2x4 slice. The times are simulated.
32 devices in a mesh: survey: 2 (over y), gz: 4 (over z), gy: 2 (over x), pat: 2 (over core).
Axes of the slice: x: 2, y: 2, z: 4, core: 2. Of those that a mesh axis runs over, the one named last changes fastest.
Arguments:
- conductivity: float32 [32, 256, 512], P(('survey', 'gz'), 'gy'), parts along dimension 0, may hold values from 0.3 to 3
- receivers: int32 [4, 3, 64], P(('survey', 'pat')), parts along dimension 0, may hold values from 0 to 511, as said below
- observed: float32 [4, 64], P(('survey', 'pat')), parts along dimension 0, may hold values from -6 to 6
- potential: float32 [2, 32, 256, 512], P('pat', ('survey', 'gz'), 'gy'), parts along dimension 1, may hold values from -6 to 6
- adjoint_prev: float32 [2, 32, 256, 512], P('pat', ('survey', 'gz'), 'gy'), parts along dimension 1, may hold values from -0.046875 to 0.046875
Outputs:
- adjoint: float32 [2, 32, 256, 512], P('pat', ('survey', 'gz'), 'gy'), parts along dimension 1
- gradient: float32 [32, 256, 512], P(('survey', 'gz'), 'gy'), parts along dimension 0
There are 2 independent parts, one for each index of `survey`. A program takes and returns all parts, laid end to end along the dimension named above; each array names one. Nothing has to cross between parts.
Inputs may be any that keep to these rules, and one draw needn't show every extreme that they name: receivers[p, 0, r], receivers[p, 1, r] and receivers[p, 2, r] are a z cell below 16, a y cell below 256 and an x cell below 512; several receivers may share a cell.
All inputs are finite; a program needn't handle non-finite values.
Results may differ from a plain program's by a relative error of at most 0.0003.
Values sent between devices are 32-bit elements; how exact they have to be, the bound alone decides.
A program may use at most 64 MiB of HBM per device.

v0:
```python
import jax
import jax.numpy as jnp
from jax import lax
from jax.sharding import PartitionSpec as P

relax_weight = 0.8


def extended_2(cells, sides, width):
    for axis, dim in sides:
        count = lax.axis_size(axis)
        ends = count - 1
        head = lax.slice_in_dim(cells, 0, width, axis=dim)
        tail = lax.slice_in_dim(cells, cells.shape[dim] - width, cells.shape[dim], axis=dim)
        cells = jnp.concatenate(
            [
                lax.ppermute(tail, axis, [(i, (i + 1) % count) for i in range(ends)]),
                cells,
                lax.ppermute(head, axis, [((i + 1) % count, i) for i in range(ends)]),
            ],
            axis=dim,
        )
    return cells


def beside_cells(extended):
    widened = jnp.pad(extended, [(0, 0)] * (extended.ndim - 1) + [(1, 1)])
    centre = widened[..., 1:-1, 1:-1, 1:-1]
    others = [
        widened[..., 2:, 1:-1, 1:-1],
        widened[..., :-2, 1:-1, 1:-1],
        widened[..., 1:-1, 2:, 1:-1],
        widened[..., 1:-1, :-2, 1:-1],
        widened[..., 1:-1, 1:-1, 2:],
        widened[..., 1:-1, 1:-1, :-2],
    ]
    return (centre, others)


def relax(cond_ext, adjoint_ext, source):
    cond_mid, cond_near = beside_cells(cond_ext)
    adj_mid, adj_near = beside_cells(adjoint_ext)
    diagonal = jnp.zeros_like(cond_mid)
    coupled = jnp.zeros_like(adj_mid)
    for cond_side, adj_side in zip(cond_near, adj_near):
        face_coef = 0.5 * (cond_mid + cond_side)
        diagonal = diagonal + face_coef
        coupled = coupled + face_coef * adj_side
    updated = adj_mid + relax_weight * (source - diagonal * adj_mid + coupled) / diagonal
    return updated


def contribution(pot_ext, adj_ext):
    pot_mid, pot_near = beside_cells(pot_ext)
    adj_mid, adj_near = beside_cells(adj_ext)
    summed = jnp.zeros_like(adj_mid)
    for pot_side, adj_side in zip(pot_near, adj_near):
        summed = summed + (pot_mid - pot_side) * (adj_mid - adj_side)
    return -0.5 * jnp.sum(summed, axis=0)


def receiver_source(field, receivers, observed, z_start, y_start):
    z_count = field.shape[1]
    y_count = field.shape[2]
    z_local = receivers[:, 0, :] - z_start
    y_local = receivers[:, 1, :] - y_start
    x_local = receivers[:, 2, :]
    inside = (z_local >= 0) & (z_local < z_count) & (y_local >= 0) & (y_local < y_count)
    z_local = jnp.clip(z_local, 0, z_count - 1)
    y_local = jnp.clip(y_local, 0, y_count - 1)
    pattern_ids = jnp.broadcast_to(
        jnp.arange(field.shape[0], dtype=jnp.int32)[:, None], z_local.shape
    )
    values = jnp.where(
        inside, field[pattern_ids, z_local, y_local, x_local] - observed, jnp.zeros_like(observed)
    )
    return jnp.zeros_like(field).at[pattern_ids, z_local, y_local, x_local].add(values)


def local(conductivity, receivers, observed, potential, adjoint_prev):
    pattern_count = potential.shape[0]
    z_cells = conductivity.shape[0]
    y_cells = conductivity.shape[1]
    z_first = lax.axis_index("gz") * z_cells
    y_first = lax.axis_index("gy") * y_cells
    stacked = jnp.concatenate([conductivity[None], adjoint_prev], axis=0)
    extended = extended_2(stacked, (("gz", 1), ("gy", 2)), 1)
    cond_ext = extended[0]
    source = receiver_source(potential, receivers, observed, z_first, y_first)
    adjoint = relax(cond_ext, extended[1:], source)
    rimmed = extended_2(adjoint, (("gz", 1), ("gy", 2)), 1)
    adjoint = relax(cond_ext, rimmed, source)
    both_ext = extended_2(jnp.concatenate([potential, adjoint], axis=0), (("gz", 1), ("gy", 2)), 1)
    partial_grad = contribution(both_ext[:pattern_count], both_ext[pattern_count:])
    gradient = lax.psum(partial_grad, "pat")
    return (adjoint, gradient)


def solution(mesh):
    return jax.shard_map(
        local,
        mesh=mesh,
        in_specs=(
            P(("survey", "gz"), "gy", None),
            P(("survey", "pat"), None, None),
            P(("survey", "pat"), None),
            P("pat", ("survey", "gz"), "gy", None),
            P("pat", ("survey", "gz"), "gy", None),
        ),
        out_specs=(P("pat", ("survey", "gz"), "gy", None), P(("survey", "gz"), "gy", None)),
        check_vma=False,
    )
```

profile of v0, /device:TPU:0, one launch (start us, length us, event | category | flops | bytes accessed | tf_op | source)
XLA Modules:
  0.0 133.2 jit_solution(9145302090978864290)
XLA Ops:
  7.2 2.4 %pad_maximum_fusion.37 = (f32[2,1,128,512]{3,2,1,0:T(8,128)}, f32[2,1,128,512]{3,2,1,0:T(8,128)}) fusion(f32[1,4,128,512]{3,2,1,0:T(8,128)} %param.9, f32[1,4,128,512]{3,2,1,0:T(8,128)} %bitcast.63), kind=kLoop, calls=%fused_computation.126 | loop fusion | flops 262144 | bytes 3145728 | tf_op jit(solution)/shard_map/slice | solution.py:14
  9.6 5.9 %collective-permute-start = (f32[2,1,128,512]{3,2,1,0:T(8,128)}, f32[2,1,128,512]{3,2,1,0:T(8,128)}, u32[]{:S(2)}, u32[]{:S(2)}) collective-permute-start(f32[2,1,128,512]{3,2,1,0:T(8,128)} %get-tuple-element.12), channel_id=1, source_target_pairs={{0,4},{4,8},{8,12},{1,5},{5,9},{9,13},{2,6},{6,10},{10,14},{3,7},{... | collective-permute-start | bytes 1572872 | tf_op jit(solution)/shard_map/ppermute | solution.py:17
  15.5 1.3 collective-permute-start.1
  16.9 1.0 gather_fusion
  17.9 8.3 %collective-permute-done = f32[2,1,128,512]{3,2,1,0:T(8,128)} collective-permute-done((f32[2,1,128,512]{3,2,1,0:T(8,128)}, f32[2,1,128,512]{3,2,1,0:T(8,128)}, u32[]{:S(2)}, u32[]{:S(2)}) %collective-permute-start) | collective-permute-done | bytes 524320 | tf_op jit(solution)/shard_map/ppermute | solution.py:17
  26.2 4.9 %collective-permute-done.1 = f32[2,1,128,512]{3,2,1,0:T(8,128)} collective-permute-done((f32[2,1,128,512]{3,2,1,0:T(8,128)}, f32[2,1,128,512]{3,2,1,0:T(8,128)}, u32[]{:S(2)}, u32[]{:S(2)}) %collective-permute-start.1) | collective-permute-done | bytes 524320 | tf_op jit(solution)/shard_map/ppermute | solution.py:19
  31.1 0.8 pad_maximum_fusion.45
  32.0 3.4 %collective-permute-start.2 = (f32[2,6,1,512]{3,2,1,0:T(1,128)S(1)}, f32[2,6,1,512]{3,2,1,0:T(1,128)S(1)}, u32[]{:S(2)}, u32[]{:S(2)}) collective-permute-start(f32[2,6,1,512]{3,2,1,0:T(1,128)S(1)} %get-tuple-element.8), channel_id=1, source_target_pairs={{0,2},{1,3},{4,6},{5,7},{8,10},{9,11},{12,14},{13,15},{16,18},{17,... | collective-permute-start | bytes 73736 | tf_op jit(solution)/shard_map/ppermute | solution.py:17
  35.4 1.3 collective-permute-start.3
  36.7 1.1 broadcast.273
  37.8 9.4 %scatter_fusion = f32[4,128,512]{2,1,0:T(8,128)} fusion(f32[4,128,512]{2,1,0:T(8,128)} %broadcast.273, s32[64]{0:T(128)S(1)} %get-tuple-element.19, f32[64]{0:T(128)S(1)} %fusion.63), kind=kCustom, calls=%fused_computation.1 | custom fusion | flops 64 | bytes 1536 | tf_op jit(solution)/shard_map/scatter-add | solution.py:77
  47.2 1.7 %pad_maximum_fusion = f32[2,6,130,512]{3,2,1,0:T(8,128)S(1)} fusion(f32[2,6,1,512]{3,2,1,0:T(1,128)S(1)} %collective-permute-done.3, f32[2,1,128,512]{3,2,1,0:T(8,128)} %collective-permute-done.1, f32[1,4,128,512]{3,2,1,0:T(8,128)S(1)} %copy-done.2, f32[1,4,128,512]{3,2,1,0:T(8,128)S(1)} %bitcast.65, f32[2,1,128,512]{3,2,1,0:T(8,128)} %collective-permute-done, ...), kind=kLoop, calls=%fused_computation.2 | loop fusion | flops 3993600 | bytes 6389760 | tf_op jit(solution)/shard_map/concatenate | solution.py:15
  49.2 0.9 copy-done.4
  50.0 4.7 %fusion.11 = f32[1,4,128,512]{3,2,1,0:T(8,128)S(1)} fusion(f32[1,4,128,512]{3,2,1,0:T(8,128)S(1)} %copy-done.2, f32[1,6,130,512]{3,2,1,0:T(8,128)S(1)} %get-tuple-element.5, f32[2,6,1,512]{3,2,1,0:T(1,128)S(1)} %collective-permute-done.2, f32[2,1,128,512]{3,2,1,0:T(8,128)} %collective-permute-done.1, f32[2,1,128,512]{3,2,1,0:T(8,128)} %collective-permute-done, ...), kind=kLoop, calls=%fused_computation.30 | loop fusion | flops 12058624 | bytes 13877248 | tf_op jit(solution)/shard_map/add | solution.py:49
  54.8 2.7 %collective-permute-start.5 = (f32[1,1,128,512]{3,2,1,0:T(8,128)S(1)}, f32[1,1,128,512]{3,2,1,0:T(8,128)S(1)}, u32[]{:S(2)}, u32[]{:S(2)}) collective-permute-start(f32[1,1,128,512]{3,2,1,0:T(8,128)S(1)} %get-tuple-element.16), channel_id=1, source_target_pairs={{0,4},{4,8},{8,12},{1,5},{5,9},{9,13},{2,6},{6,10},{10,14},{3,7},{... | collective-permute-start | bytes 786440 | tf_op jit(solution)/shard_map/ppermute | solution.py:17
  57.5 1.3 collective-permute-start.4
  58.8 2.8 %collective-permute-done.5 = f32[1,1,128,512]{3,2,1,0:T(8,128)S(1)} collective-permute-done((f32[1,1,128,512]{3,2,1,0:T(8,128)S(1)}, f32[1,1,128,512]{3,2,1,0:T(8,128)S(1)}, u32[]{:S(2)}, u32[]{:S(2)}) %collective-permute-start.5) | collective-permute-done | bytes 262176 | tf_op jit(solution)/shard_map/ppermute | solution.py:17
  61.6 4.2 %collective-permute-done.4 = f32[1,1,128,512]{3,2,1,0:T(8,128)S(1)} collective-permute-done((f32[1,1,128,512]{3,2,1,0:T(8,128)S(1)}, f32[1,1,128,512]{3,2,1,0:T(8,128)S(1)}, u32[]{:S(2)}, u32[]{:S(2)}) %collective-permute-start.4) | collective-permute-done | bytes 262176 | tf_op jit(solution)/shard_map/ppermute | solution.py:19
  65.8 4.5 %collective-permute-start.7 = (f32[1,6,1,512]{3,2,1,0:T(1,128)S(1)}, f32[1,6,1,512]{3,2,1,0:T(1,128)S(1)}, u32[]{:S(2)}, u32[]{:S(2)}) collective-permute-start(f32[1,6,1,512]{3,2,1,0:T(1,128)S(1)} %get-tuple-element.14), channel_id=1, source_target_pairs={{0,2},{1,3},{4,6},{5,7},{8,10},{9,11},{12,14},{13,15},{16,18},{17,... | collective-permute-start | bytes 36872 | tf_op jit(solution)/shard_map/ppermute | solution.py:17
  70.3 1.3 collective-permute-start.6
  71.7 4.2 %collective-permute-done.6 = f32[1,6,1,512]{3,2,1,0:T(1,128)S(1)} collective-permute-done((f32[1,6,1,512]{3,2,1,0:T(1,128)S(1)}, f32[1,6,1,512]{3,2,1,0:T(1,128)S(1)}, u32[]{:S(2)}, u32[]{:S(2)}) %collective-permute-start.6) | collective-permute-done | bytes 12320 | tf_op jit(solution)/shard_map/ppermute | solution.py:19
  76.6 3.4 %fusion.38 = f32[1,4,128,512]{3,2,1,0:T(8,128)S(1)} fusion(f32[1,4,128,512]{3,2,1,0:T(8,128)S(1)} %fusion.11, f32[1,6,130,514]{3,2,1,0:T(8,128)S(1)} %select_maximum_fusion, f32[1,6,1,512]{3,2,1,0:T(1,128)S(1)} %collective-permute-done.7, f32[1,1,128,512]{3,2,1,0:T(8,128)S(1)} %collective-permute-done.4, f32[1,1,128,512]{3,2,1,0:T(8,128)S(1)} %collective-permute-done.5, ...), kind=kLoop, calls=%fused_computation.74 | loop fusion | flops 11010048 | bytes 12705792 | tf_op jit(solution)/shard_map/add | solution.py:49
  80.2 3.5 %collective-permute-start.9 = (f32[2,1,128,512]{3,2,1,0:T(8,128)S(1)}, f32[2,1,128,512]{3,2,1,0:T(8,128)S(1)}, u32[]{:S(2)}, u32[]{:S(2)}) collective-permute-start(f32[2,1,128,512]{3,2,1,0:T(8,128)S(1)} %get-tuple-element.10), channel_id=1, source_target_pairs={{0,4},{4,8},{8,12},{1,5},{5,9},{9,13},{2,6},{6,10},{10,14},{3,7},{... | collective-permute-start | bytes 1572872 | tf_op jit(solution)/shard_map/ppermute | solution.py:17
  83.7 1.3 collective-permute-start.8
  85.0 5.3 %collective-permute-done.9 = f32[2,1,128,512]{3,2,1,0:T(8,128)S(1)} collective-permute-done((f32[2,1,128,512]{3,2,1,0:T(8,128)S(1)}, f32[2,1,128,512]{3,2,1,0:T(8,128)S(1)}, u32[]{:S(2)}, u32[]{:S(2)}) %collective-permute-start.9) | collective-permute-done | bytes 524320 | tf_op jit(solution)/shard_map/ppermute | solution.py:17
  90.3 4.4 %collective-permute-done.8 = f32[2,1,128,512]{3,2,1,0:T(8,128)S(1)} collective-permute-done((f32[2,1,128,512]{3,2,1,0:T(8,128)S(1)}, f32[2,1,128,512]{3,2,1,0:T(8,128)S(1)}, u32[]{:S(2)}, u32[]{:S(2)}) %collective-permute-start.8) | collective-permute-done | bytes 524320 | tf_op jit(solution)/shard_map/ppermute | solution.py:19
  94.8 1.6 %collective-permute-start.11 = (f32[2,6,1,512]{3,2,1,0:T(1,128)S(1)}, f32[2,6,1,512]{3,2,1,0:T(1,128)S(1)}, u32[]{:S(2)}, u32[]{:S(2)}) collective-permute-start(f32[2,6,1,512]{3,2,1,0:T(1,128)S(1)} %get-tuple-element.6), channel_id=1, source_target_pairs={{0,2},{1,3},{4,6},{5,7},{8,10},{9,11},{12,14},{13,15},{16,18},{17,... | collective-permute-start | bytes 73736 | tf_op jit(solution)/shard_map/ppermute | solution.py:17
  96.4 1.3 collective-permute-start.10
  97.9 4.2 %collective-permute-done.10 = f32[2,6,1,512]{3,2,1,0:T(1,128)S(1)} collective-permute-done((f32[2,6,1,512]{3,2,1,0:T(1,128)S(1)}, f32[2,6,1,512]{3,2,1,0:T(1,128)S(1)}, u32[]{:S(2)}, u32[]{:S(2)}) %collective-permute-start.10) | collective-permute-done | bytes 24608 | tf_op jit(solution)/shard_map/ppermute | solution.py:19
  103.0 4.3 %fusion.18 = f32[4,128,512]{2,1,0:T(8,128)} fusion(f32[1,4,128,512]{3,2,1,0:T(8,128)S(1)} %copy-done.1, f32[1,6,130,512]{3,2,1,0:T(8,128)S(1)} %get-tuple-element.3, f32[1,4,128,512]{3,2,1,0:T(8,128)S(1)} %fusion.38, f32[1,6,130,512]{3,2,1,0:T(8,128)S(1)} %get-tuple-element.2, f32[2,6,1,512]{3,2,1,0:T(1,128)S(1)} %collective-permute-done.11, ...), kind=kLoop, calls=%fused_computation.37 | loop fusion | flops 12582912 | bytes 7438336 | tf_op jit(solution)/shard_map/mul | solution.py:59
  107.3 16.9 %all-reduce.7.cloned.1.call-done = f32[4,128,512]{2,1,0:T(8,128)} async-done(((f32[4,128,512]{2,1,0:T(8,128)}), f32[4,128,512]{2,1,0:T(8,128)}) %all-reduce.7.cloned.1.call-update) | async-done | bytes 1048592 | tf_op jit(solution)/shard_map/psum | solution.py:95
  124.1 2.3 %copy.9 = f32[4,128,512]{2,1,0:T(8,128)} copy(f32[4,128,512]{2,1,0:T(8,128)} %all-reduce.7.cloned.1.call-done) | data formatting | bytes 2097152
  (32 shorter events, 2.5 us)
Async XLA Ops:
  7.2 23.9 %copy-start.2 = (f32[1,4,128,512]{3,2,1,0:T(8,128)S(1)}, f32[1,4,128,512]{3,2,1,0:T(8,128)}, u32[]{:S(2)}) copy-start(f32[1,4,128,512]{3,2,1,0:T(8,128)} %param.9) | copy-start | bytes 3145732
  7.2 23.9 %copy-start.3 = (f32[4,128,512]{2,1,0:T(8,128)S(1)}, f32[4,128,512]{2,1,0:T(8,128)}, u32[]{:S(2)}) copy-start(f32[4,128,512]{2,1,0:T(8,128)} %param.5) | copy-start | bytes 3145732
  7.2 9.6 %copy-start.5 = (s32[1,3,64]{2,0,1:T(1,128)S(1)}, s32[1,3,64]{2,0,1:T(1,128)}, u32[]{:S(2)}) copy-start(s32[1,3,64]{2,0,1:T(1,128)} %param.6) | copy-start | bytes 2308
  7.2 9.7 %copy-start.1 = (f32[1,4,128,512]{3,2,1,0:T(8,128)S(1)}, f32[1,4,128,512]{3,2,1,0:T(8,128)}, u32[]{:S(2)}) copy-start(f32[1,4,128,512]{3,2,1,0:T(8,128)} %param.8) | copy-start | bytes 3145732
  7.2 116.9 %all-reduce.7.cloned.1.call-start = ((), (), s32[]{:S(2)}) async-start(), calls=%async_computation | async-start | bytes 2097152 | tf_op jit(solution)/shard_map/psum | solution.py:95
  9.6 27.0 %copy-start.6 = (f32[1,64]{1,0:T(1,128)S(1)}, f32[1,64]{1,0:T(1,128)}, u32[]{:S(2)}) copy-start(f32[1,64]{1,0:T(1,128)} %param.7) | copy-start | bytes 772
  9.6 16.6 %collective-permute-start = (f32[2,1,128,512]{3,2,1,0:T(8,128)}, f32[2,1,128,512]{3,2,1,0:T(8,128)}, u32[]{:S(2)}, u32[]{:S(2)}) collective-permute-start(f32[2,1,128,512]{3,2,1,0:T(8,128)} %get-tuple-element.12), channel_id=1, source_target_pairs={{0,4},{4,8},{8,12},{1,5},{5,9},{9,13},{2,6},{6,10},{10,14},{3,7},{... | collective-permute-start | bytes 1572872 | tf_op jit(solution)/shard_map/ppermute | solution.py:17
  15.5 15.6 %collective-permute-start.1 = (f32[2,1,128,512]{3,2,1,0:T(8,128)}, f32[2,1,128,512]{3,2,1,0:T(8,128)}, u32[]{:S(2)}, u32[]{:S(2)}) collective-permute-start(f32[2,1,128,512]{3,2,1,0:T(8,128)} %get-tuple-element.13), channel_id=1, source_target_pairs={{4,0},{8,4},{12,8},{5,1},{9,5},{13,9},{6,2},{10,6},{14,10},{7,3},{... | collective-permute-start | bytes 1572872 | tf_op jit(solution)/shard_map/ppermute | solution.py:19
  32.0 15.2 %collective-permute-start.2 = (f32[2,6,1,512]{3,2,1,0:T(1,128)S(1)}, f32[2,6,1,512]{3,2,1,0:T(1,128)S(1)}, u32[]{:S(2)}, u32[]{:S(2)}) collective-permute-start(f32[2,6,1,512]{3,2,1,0:T(1,128)S(1)} %get-tuple-element.8), channel_id=1, source_target_pairs={{0,2},{1,3},{4,6},{5,7},{8,10},{9,11},{12,14},{13,15},{16,18},{17,... | collective-permute-start | bytes 73736 | tf_op jit(solution)/shard_map/ppermute | solution.py:17
  35.4 11.8 %collective-permute-start.3 = (f32[2,6,1,512]{3,2,1,0:T(1,128)S(1)}, f32[2,6,1,512]{3,2,1,0:T(1,128)S(1)}, u32[]{:S(2)}, u32[]{:S(2)}) collective-permute-start(f32[2,6,1,512]{3,2,1,0:T(1,128)S(1)} %get-tuple-element.9), channel_id=1, source_target_pairs={{2,0},{3,1},{6,4},{7,5},{10,8},{11,9},{14,12},{15,13},{18,16},{19,... | collective-permute-start | bytes 73736 | tf_op jit(solution)/shard_map/ppermute | solution.py:19
  48.8 1.2 copy-start.4
  54.8 6.8 %collective-permute-start.5 = (f32[1,1,128,512]{3,2,1,0:T(8,128)S(1)}, f32[1,1,128,512]{3,2,1,0:T(8,128)S(1)}, u32[]{:S(2)}, u32[]{:S(2)}) collective-permute-start(f32[1,1,128,512]{3,2,1,0:T(8,128)S(1)} %get-tuple-element.16), channel_id=1, source_target_pairs={{0,4},{4,8},{8,12},{1,5},{5,9},{9,13},{2,6},{6,10},{10,14},{3,7},{... | collective-permute-start | bytes 786440 | tf_op jit(solution)/shard_map/ppermute | solution.py:17
  57.5 8.3 %collective-permute-start.4 = (f32[1,1,128,512]{3,2,1,0:T(8,128)S(1)}, f32[1,1,128,512]{3,2,1,0:T(8,128)S(1)}, u32[]{:S(2)}, u32[]{:S(2)}) collective-permute-start(f32[1,1,128,512]{3,2,1,0:T(8,128)S(1)} %get-tuple-element.17), channel_id=1, source_target_pairs={{4,0},{8,4},{12,8},{5,1},{9,5},{13,9},{6,2},{10,6},{14,10},{7,3},{... | collective-permute-start | bytes 786440 | tf_op jit(solution)/shard_map/ppermute | solution.py:19
  65.8 5.9 %collective-permute-start.7 = (f32[1,6,1,512]{3,2,1,0:T(1,128)S(1)}, f32[1,6,1,512]{3,2,1,0:T(1,128)S(1)}, u32[]{:S(2)}, u32[]{:S(2)}) collective-permute-start(f32[1,6,1,512]{3,2,1,0:T(1,128)S(1)} %get-tuple-element.14), channel_id=1, source_target_pairs={{0,2},{1,3},{4,6},{5,7},{8,10},{9,11},{12,14},{13,15},{16,18},{17,... | collective-permute-start | bytes 36872 | tf_op jit(solution)/shard_map/ppermute | solution.py:17
  70.3 5.6 %collective-permute-start.6 = (f32[1,6,1,512]{3,2,1,0:T(1,128)S(1)}, f32[1,6,1,512]{3,2,1,0:T(1,128)S(1)}, u32[]{:S(2)}, u32[]{:S(2)}) collective-permute-start(f32[1,6,1,512]{3,2,1,0:T(1,128)S(1)} %get-tuple-element.15), channel_id=1, source_target_pairs={{2,0},{3,1},{6,4},{7,5},{10,8},{11,9},{14,12},{15,13},{18,16},{19,... | collective-permute-start | bytes 36872 | tf_op jit(solution)/shard_map/ppermute | solution.py:19
  80.1 22.9 %copy-start = (f32[1,4,128,512]{3,2,1,0:T(8,128)}, f32[1,4,128,512]{3,2,1,0:T(8,128)S(1)}, u32[]{:S(2)}) copy-start(f32[1,4,128,512]{3,2,1,0:T(8,128)S(1)} %fusion.38) | copy-start | bytes 3145732
  80.2 10.2 %collective-permute-start.9 = (f32[2,1,128,512]{3,2,1,0:T(8,128)S(1)}, f32[2,1,128,512]{3,2,1,0:T(8,128)S(1)}, u32[]{:S(2)}, u32[]{:S(2)}) collective-permute-start(f32[2,1,128,512]{3,2,1,0:T(8,128)S(1)} %get-tuple-element.10), channel_id=1, source_target_pairs={{0,4},{4,8},{8,12},{1,5},{5,9},{9,13},{2,6},{6,10},{10,14},{3,7},{... | collective-permute-start | bytes 1572872 | tf_op jit(solution)/shard_map/ppermute | solution.py:17
  83.7 11.1 %collective-permute-start.8 = (f32[2,1,128,512]{3,2,1,0:T(8,128)S(1)}, f32[2,1,128,512]{3,2,1,0:T(8,128)S(1)}, u32[]{:S(2)}, u32[]{:S(2)}) collective-permute-start(f32[2,1,128,512]{3,2,1,0:T(8,128)S(1)} %get-tuple-element.11), channel_id=1, source_target_pairs={{4,0},{8,4},{12,8},{5,1},{9,5},{13,9},{6,2},{10,6},{14,10},{7,3},{... | collective-permute-start | bytes 1572872 | tf_op jit(solution)/shard_map/ppermute | solution.py:19
  94.8 3.2 %collective-permute-start.11 = (f32[2,6,1,512]{3,2,1,0:T(1,128)S(1)}, f32[2,6,1,512]{3,2,1,0:T(1,128)S(1)}, u32[]{:S(2)}, u32[]{:S(2)}) collective-permute-start(f32[2,6,1,512]{3,2,1,0:T(1,128)S(1)} %get-tuple-element.6), channel_id=1, source_target_pairs={{0,2},{1,3},{4,6},{5,7},{8,10},{9,11},{12,14},{13,15},{16,18},{17,... | collective-permute-start | bytes 73736 | tf_op jit(solution)/shard_map/ppermute | solution.py:17
  96.4 5.7 %collective-permute-start.10 = (f32[2,6,1,512]{3,2,1,0:T(1,128)S(1)}, f32[2,6,1,512]{3,2,1,0:T(1,128)S(1)}, u32[]{:S(2)}, u32[]{:S(2)}) collective-permute-start(f32[2,6,1,512]{3,2,1,0:T(1,128)S(1)} %get-tuple-element.7), channel_id=1, source_target_pairs={{2,0},{3,1},{6,4},{7,5},{10,8},{11,9},{14,12},{15,13},{18,16},{19,... | collective-permute-start | bytes 73736 | tf_op jit(solution)/shard_map/ppermute | solution.py:19
Sparse Core Ops, SparseCore 0:
  107.4 16.7 all-reduce.6
where the time goes:
time: 134 us; the launch traced here: 133 us
  waiting for transfers between devices  55.5 us (41%)
  starting transfers between devices  29.4 us (22%)
  other arithmetic  27.9 us (21%)
  between operations  14.3 us (11%)
  local copies, waits for them, and re-layouts  5.99 us (4%)
    ppermute x6, waiting for transfers between devices, extended_2(): lax.ppermute(head, axis, [((i + 1) % count, i) for i in range(ends)])  21.9 us
    ppermute x6, starting transfers between devices, extended_2(): lax.ppermute(tail, axis, [(i, (i + 1) % count) for i in range(ends)])  21.7 us
    psum x1, waiting for transfers between devices, local(): gradient = lax.psum(partial_grad, 'pat')  16.9 us
    ppermute x6, waiting for transfers between devices, extended_2(): lax.ppermute(tail, axis, [(i, (i + 1) % count) for i in range(ends)])  16.7 us
    scatter-add x1, other arithmetic, receiver_source(): jnp.zeros_like(field).at[pattern_ids, z_local, y_local, x_local].add(values)  9.37 us
    add x2, other arithmetic, relax(): adj_mid + relax_weight * (source - diagonal * adj_mid + coupled) / diagonal  8.09 us
    ppermute x6, starting transfers between devices, extended_2(): lax.ppermute(head, axis, [((i + 1) % count, i) for i in range(ends)])  7.74 us
    mul x1, other arithmetic, contribution(): return -0.5 * jnp.sum(summed, axis=0)  4.25 us
  transfers between devices with their start and end apart: 13, of which 11 were waited for; matrix products, arithmetic and copies ran while one was open for 9% of the time, Pallas kernels for 0%

commit v1 on v0

v1 whole, which is shorter than its diff:
```python
import functools

import jax
import jax.numpy as jnp
from jax import lax
from jax.experimental import pallas as pl
from jax.experimental.pallas import tpu as pltpu
from jax.sharding import PartitionSpec as P

relax_weight = 0.8
MESH = pl.DeviceIdType.MESH
PAD = 8
CHUNKS = 4
COND, ADJ0, POT, ADJ1, ADJ2 = range(5)
UP, DOWN = 0, 1
HIGH = lax.Precision.HIGHEST


def kernel(
    counts,
    cond_hbm,
    recv_ref,
    obs_ref,
    pot_hbm,
    adj_hbm,
    adj_out,
    grad_out,
    cond,
    adj0,
    pot,
    adj1,
    adj2,
    source,
    weight,
    grad,
    grad_far,
    load_sem,
    out_sem,
    z_send,
    z_recv,
    y_send,
    y_recv,
    relay_send,
    relay_recv,
    g_send,
    g_recv,
):
    gz_count, gy_count = counts
    planes, rows, lanes = cond_hbm.shape
    top = planes + 1
    chunk = rows // CHUNKS
    half = rows // 2
    gz = lax.axis_index("gz")
    gy = lax.axis_index("gy")
    pat = lax.axis_index("pat")
    partner = 1 - pat
    z_has = (gz < gz_count - 1, gz > 0)
    z_from = (gz > 0, gz < gz_count - 1)
    z_to = ({"gz": gz + 1}, {"gz": gz - 1})
    y_has = (gy < gy_count - 1, gy > 0)
    y_from = (gy > 0, gy < gy_count - 1)
    y_to = ({"gy": gy + 1}, {"gy": gy - 1})
    inside = pl.ds(PAD, rows)

    hbm_of = {COND: cond_hbm, ADJ0: adj_hbm.at[0], POT: pot_hbm.at[0]}
    vmem_of = {COND: cond, ADJ0: adj0, POT: pot, ADJ1: adj1, ADJ2: adj2}

    loads = []
    for field in (COND, ADJ0, POT):
        loads.append(
            pltpu.make_async_copy(
                hbm_of[field], vmem_of[field].at[pl.ds(1, planes), inside], load_sem.at[field]
            )
        )
    for copy in loads:
        copy.start()

    barrier = pltpu.get_barrier_semaphore()
    for way in (UP, DOWN):

        @pl.when(z_has[way])
        def _():
            pl.semaphore_signal(barrier, inc=1, device_id=z_to[way], device_id_type=MESH)

        @pl.when(y_has[way])
        def _():
            pl.semaphore_signal(barrier, inc=1, device_id=y_to[way], device_id_type=MESH)

    pl.semaphore_signal(barrier, inc=1, device_id={"pat": partner}, device_id_type=MESH)

    for field in range(5):
        buf = vmem_of[field]
        for way in (UP, DOWN):

            @pl.when(jnp.logical_not(z_from[way]))
            def _():
                buf[0 if way == UP else top, PAD : PAD + rows] = jnp.zeros((rows, lanes), jnp.float32)

            @pl.when(jnp.logical_not(y_from[way]))
            def _():
                at = 0 if way == UP else PAD + rows
                buf[1:top, at : at + PAD] = jnp.zeros((planes, PAD, lanes), jnp.float32)

    neighbours = (
        1
        + z_has[0].astype(jnp.int32)
        + z_has[1].astype(jnp.int32)
        + y_has[0].astype(jnp.int32)
        + y_has[1].astype(jnp.int32)
    )
    pl.semaphore_wait(barrier, neighbours)

    def z_copy(field, way, part):
        buf = vmem_of[field]
        ghost = 0 if way == UP else top
        if field == COND:
            start, count = pl.multiple_of(pat * half, 8), half
        else:
            start, count = part * chunk, chunk
        if field in hbm_of:
            src = hbm_of[field].at[planes - 1 if way == UP else 0, pl.ds(start, count)]
        else:
            src = buf.at[planes if way == UP else 1, pl.ds(PAD + start, count)]
        return pltpu.make_async_remote_copy(
            src_ref=src,
            dst_ref=buf.at[ghost, pl.ds(PAD + start, count)],
            send_sem=z_send.at[field, way, part],
            recv_sem=z_recv.at[field, way, part],
            device_id=z_to[way],
            device_id_type=MESH,
        )

    def y_copy(field, way):
        buf = vmem_of[field]
        ghost = 0 if way == UP else PAD + rows
        if field in hbm_of:
            src = hbm_of[field].at[:, pl.ds(rows - PAD if way == UP else 0, PAD)]
        else:
            src = buf.at[pl.ds(1, planes), pl.ds(rows if way == UP else PAD, PAD)]
        return pltpu.make_async_remote_copy(
            src_ref=src,
            dst_ref=buf.at[pl.ds(1, planes), pl.ds(ghost, PAD)],
            send_sem=y_send.at[field, way],
            recv_sem=y_recv.at[field, way],
            device_id=y_to[way],
            device_id_type=MESH,
        )

    def relay(way):
        at = cond.at[0 if way == UP else top, pl.ds(pl.multiple_of(PAD + pat * half, 8), half)]
        return pltpu.make_async_remote_copy(
            src_ref=at,
            dst_ref=at,
            send_sem=relay_send.at[way],
            recv_sem=relay_recv.at[way],
            device_id={"pat": partner},
            device_id_type=MESH,
        )

    def g_copy(part):
        plane = part // CHUNKS
        at = pl.ds((part % CHUNKS) * chunk, chunk)
        return pltpu.make_async_remote_copy(
            src_ref=grad.at[plane, at],
            dst_ref=grad_far.at[plane, at],
            send_sem=g_send.at[part],
            recv_sem=g_recv.at[part],
            device_id={"pat": partner},
            device_id_type=MESH,
        )

    def guarded(flag, action):
        @pl.when(flag)
        def _():
            action()

    def start_z(field, way, part):
        guarded(z_has[way], lambda: z_copy(field, way, part).start())

    def wait_z(field, way, part):
        guarded(z_from[way], lambda: z_copy(field, way, part).wait_recv())

    def start_y(field):
        for way in (UP, DOWN):
            guarded(y_has[way], lambda: y_copy(field, way).start())

    def wait_y(field):
        for way in (UP, DOWN):
            guarded(y_from[way], lambda: y_copy(field, way).wait_recv())

    for way in (UP, DOWN):
        start_z(COND, way, 0)
    for part in range(CHUNKS):
        for way in (UP, DOWN):
            start_z(ADJ0, way, part)
    for field in (COND, ADJ0, POT):
        start_y(field)

    for copy in loads:
        copy.wait()

    recv_count = recv_ref.shape[-1]
    z_at = recv_ref[0, 0:1, :] - gz * planes
    y_at = recv_ref[0, 1:2, :] - gy * rows
    near = (z_at >= 0) & (z_at < planes) & (y_at >= 0) & (y_at < rows)
    line = jnp.where(near, z_at * rows + y_at, -1)
    eye = lax.broadcasted_iota(jnp.int32, (recv_count, recv_count), 0) == lax.broadcasted_iota(
        jnp.int32, (recv_count, recv_count), 1
    )

    def column(row):
        wide = jnp.broadcast_to(row.astype(jnp.float32), (recv_count, recv_count))
        return jnp.sum(jnp.where(eye, wide, 0.0), axis=1, keepdims=True)

    line_col = column(line).astype(jnp.int32)
    x_col = column(recv_ref[0, 2:3, :]).astype(jnp.int32)
    obs_col = column(obs_ref[...])
    picked = jnp.zeros((recv_count, lanes), jnp.float32)
    along = lax.broadcasted_iota(jnp.int32, (recv_count, rows), 1)
    for plane in range(planes):
        hot = jnp.where(along + plane * rows == line_col, 1.0, 0.0)
        picked = picked + jnp.dot(
            hot, pot[plane + 1, PAD : PAD + rows], precision=HIGH, preferred_element_type=jnp.float32
        )
    at_x = lax.broadcasted_iota(jnp.int32, (recv_count, lanes), 1) == x_col
    value = jnp.sum(jnp.where(at_x, picked, 0.0), axis=1, keepdims=True) - obs_col
    value = jnp.where(line_col >= 0, value, 0.0)
    spread = jnp.where(at_x, jnp.broadcast_to(value, at_x.shape), 0.0)
    down_rows = lax.broadcasted_iota(jnp.int32, (rows, recv_count), 0)
    for plane in range(planes):
        hot = jnp.where(down_rows + plane * rows == line, 1.0, 0.0)
        source[plane] = jnp.dot(hot, spread, precision=HIGH, preferred_element_type=jnp.float32)

    lane = lax.broadcasted_iota(jnp.int32, (8, lanes), 1)
    at_left = lane == 0
    at_right = lane == lanes - 1

    def left_of(v):
        return jnp.where(at_left, 0.0, pltpu.roll(v, 1, 1))

    def right_of(v):
        return jnp.where(at_right, 0.0, pltpu.roll(v, lanes - 1, 1))

    sub = lax.broadcasted_iota(jnp.int32, (8, lanes), 0)

    def beside(buf, plane, r, middle):
        before = buf[plane, pl.ds(pl.multiple_of(r - 8, 8), 8)]
        after = buf[plane, pl.ds(pl.multiple_of(r + 8, 8), 8)]
        return (
            pltpu.roll(jnp.where(sub == 7, before, middle), 1, 0),
            pltpu.roll(jnp.where(sub == 0, after, middle), 7, 0),
            buf[plane - 1, pl.ds(r, 8)],
            buf[plane + 1, pl.ds(r, 8)],
        )

    def relax_block(old, new, plane, r, first):
        c = cond[plane, pl.ds(r, 8)]
        a = old[plane, pl.ds(r, 8)]
        q = c * a
        sum_a = left_of(a) + right_of(a)
        sum_q = left_of(q) + right_of(q)
        if first:
            sum_c = left_of(c) + right_of(c)
        for c_n, a_n in zip(beside(cond, plane, r, c), beside(old, plane, r, a)):
            sum_a = sum_a + a_n
            sum_q = sum_q + c_n * a_n
            if first:
                sum_c = sum_c + c_n
        if first:
            diag = 3.0 * c + 0.5 * sum_c
            w = relax_weight / diag
            weight[plane - 1, pl.ds(pl.multiple_of(r - PAD, 8), 8)] = w
        else:
            w = weight[plane - 1, pl.ds(pl.multiple_of(r - PAD, 8), 8)]
        s = source[plane - 1, pl.ds(pl.multiple_of(r - PAD, 8), 8)]
        coupled = 0.5 * (c * sum_a + sum_q)
        new[plane, pl.ds(r, 8)] = (1.0 - relax_weight) * a + w * (s + coupled)

    def grad_block(plane, r):
        p = pot[plane, pl.ds(r, 8)]
        a = adj2[plane, pl.ds(r, 8)]
        total = (p - left_of(p)) * (a - left_of(a)) + (p - right_of(p)) * (a - right_of(a))
        for p_n, a_n in zip(beside(pot, plane, r, p), beside(adj2, plane, r, a)):
            total = total + (p - p_n) * (a - a_n)
        grad[plane - 1, pl.ds(pl.multiple_of(r - PAD, 8), 8)] = -0.5 * total

    def over_rows(first_row, count, action):
        def body(i, carry):
            action(pl.multiple_of(PAD + first_row + i * 8, 8))
            return carry

        lax.fori_loop(0, count // 8, body, 0)

    inner = list(range(2, planes))
    edges = [(1, UP), (planes, DOWN)]

    wait_y(COND)
    wait_y(ADJ0)
    for plane in inner:
        over_rows(0, rows, lambda r: relax_block(adj0, adj1, plane, r, True))
    for way in (UP, DOWN):

        def pass_on():
            z_copy(COND, way, 0).wait_recv()
            relay(way).start()

        guarded(z_from[way], pass_on)
    for way in (UP, DOWN):
        guarded(z_from[way], lambda: relay(way).wait())
    for part in range(CHUNKS):
        for plane, way in edges:
            wait_z(ADJ0, way, part)
            over_rows(part * chunk, chunk, lambda r: relax_block(adj0, adj1, plane, r, True))
            start_z(ADJ1, 1 - way, part)
    start_y(ADJ1)
    for part in range(CHUNKS):
        for way in (UP, DOWN):
            start_z(POT, way, part)

    wait_y(ADJ1)
    for plane in inner:
        over_rows(0, rows, lambda r: relax_block(adj1, adj2, plane, r, False))
    for part in range(CHUNKS):
        for plane, way in edges:
            wait_z(ADJ1, way, part)
            over_rows(part * chunk, chunk, lambda r: relax_block(adj1, adj2, plane, r, False))
            start_z(ADJ2, 1 - way, part)
    start_y(ADJ2)
    adj_store = pltpu.make_async_copy(
        adj2.at[pl.ds(1, planes), inside], adj_out.at[0], out_sem.at[0]
    )
    adj_store.start()

    wait_y(POT)
    wait_y(ADJ2)
    sent = []
    for plane in inner:
        over_rows(0, rows, lambda r: grad_block(plane, r))
        for part in range(CHUNKS):
            sent.append((plane - 1) * CHUNKS + part)
            g_copy(sent[-1]).start()
    for part in range(CHUNKS):
        for plane, way in edges:
            wait_z(POT, way, part)
            wait_z(ADJ2, way, part)
            over_rows(part * chunk, chunk, lambda r: grad_block(plane, r))
            sent.append((plane - 1) * CHUNKS + part)
            g_copy(sent[-1]).start()
    stores = []
    for part in sent:
        plane, start = part // CHUNKS, (part % CHUNKS) * chunk
        at = pl.ds(start, chunk)
        g_copy(part).wait_recv()
        grad_far[plane, at] = grad_far[plane, at] + grad[plane, at]
        stores.append(
            pltpu.make_async_copy(
                grad_far.at[plane, at], grad_out.at[plane, at], out_sem.at[1 + part]
            )
        )
        stores[-1].start()

    for part in sent:
        g_copy(part).wait_send()
    for way in (UP, DOWN):

        def z_done():
            z_copy(COND, way, 0).wait_send()
            for field in (ADJ0, POT, ADJ1, ADJ2):
                for part in range(CHUNKS):
                    z_copy(field, way, part).wait_send()

        def y_done():
            for field in range(5):
                y_copy(field, way).wait_send()

        guarded(z_has[way], z_done)
        guarded(y_has[way], y_done)
    adj_store.wait()
    for store in stores:
        store.wait()


def local(counts, conductivity, receivers, observed, potential, adjoint_prev):
    planes, rows, lanes = conductivity.shape
    wide = pltpu.VMEM((planes + 2, rows + 2 * PAD, lanes), jnp.float32)
    body = pltpu.VMEM((planes, rows, lanes), jnp.float32)
    dma = pltpu.SemaphoreType.DMA
    anywhere = pl.BlockSpec(memory_space=pl.ANY)
    in_vmem = pl.BlockSpec(memory_space=pltpu.VMEM)
    return pl.pallas_call(
        functools.partial(kernel, counts),
        out_shape=(
            jax.ShapeDtypeStruct(adjoint_prev.shape, jnp.float32),
            jax.ShapeDtypeStruct(conductivity.shape, jnp.float32),
        ),
        in_specs=[anywhere, in_vmem, in_vmem, anywhere, anywhere],
        out_specs=(anywhere, anywhere),
        scratch_shapes=[wide] * 5
        + [body] * 4
        + [
            dma((3,)),
            dma((1 + planes * CHUNKS,)),
            dma((5, 2, CHUNKS)),
            dma((5, 2, CHUNKS)),
            dma((5, 2)),
            dma((5, 2)),
            dma((2,)),
            dma((2,)),
            dma((planes * CHUNKS,)),
            dma((planes * CHUNKS,)),
        ],
        compiler_params=pltpu.CompilerParams(
            collective_id=0, has_side_effects=True, vmem_limit_bytes=40 * 1024 * 1024
        ),
    )(conductivity, receivers, observed, potential, adjoint_prev)


def solution(mesh):
    counts = (mesh.shape["gz"], mesh.shape["gy"])
    return jax.shard_map(
        functools.partial(local, counts),
        mesh=mesh,
        in_specs=(
            P(("survey", "gz"), "gy", None),
            P(("survey", "pat"), None, None),
            P(("survey", "pat"), None),
            P("pat", ("survey", "gz"), "gy", None),
            P("pat", ("survey", "gz"), "gy", None),
        ),
        out_specs=(P("pat", ("survey", "gz"), "gy", None), P(("survey", "gz"), "gy", None)),
        check_vma=False,
    )
```

time: 134 us -> 45.8 us (0.34)
  waiting for transfers between devices: 55.5 us -> 0 us
  Pallas kernels: 0 us -> 38.6 us
  starting transfers between devices: 29.4 us -> 0 us
  other arithmetic: 27.9 us -> 0 us
  between operations: 14.3 us -> 0.65 us
    ppermute x12 -> x0, waiting for transfers between devices: 38.7 us -> none  [the longest x6 21.9 us: extended_2(): lax.ppermute(head, axis, [((i + 1) % count, i) for i in range(ends)])]
    pallas_call x0 -> x1, Pallas kernels: none -> 38.6 us  [local(): pl.pallas_call(functools.partial(kernel, counts), out_shape=(jax.ShapeDty...]
    ppermute x12 -> x0, starting transfers between devices: 29.4 us -> none  [the longest x6 21.7 us: extended_2(): lax.ppermute(tail, axis, [(i, (i + 1) % count) for i in range(ends)])]
    psum x1 -> x0, waiting for transfers between devices: 16.9 us -> none  [local(): gradient = lax.psum(partial_grad, 'pat')]
    scatter-add x1 -> x0, other arithmetic: 9.37 us -> none  [receiver_source(): jnp.zeros_like(field).at[pattern_ids, z_local, y_local, x_local].add(values)]
    add x2 -> x0, other arithmetic: 8.09 us -> none  [relax(): adj_mid + relax_weight * (source - diagonal * adj_mid + coupled) / diagonal]
    mul x1 -> x0, other arithmetic: 4.25 us -> none  [contribution(): return -0.5 * jnp.sum(summed, axis=0)]
    slice x2 -> x0, other arithmetic: 3.22 us -> none  [extended_2(): lax.slice_in_dim(cells, cells.shape[dim] - width, cells.shape[dim], axis=...]
  transfers between devices with their start and end apart: 13 -> 0, of which waited for: 11 -> 0; matrix products, arithmetic and copies ran while one was open for 9% -> 0% of each run, Pallas kernels for 0% -> 0%
where the time goes in v1:
time: 45.8 us; the launch traced here: 45.5 us
  Pallas kernels  38.6 us (84%)
  local copies, waits for them, and re-layouts  6.31 us (14%)
  between operations  0.65 us (1%)
    pallas_call x1, Pallas kernels, local(): pl.pallas_call(functools.partial(kernel, counts), out_shape=(jax.ShapeDty...  38.6 us
    unnamed x11, local copies, waits for them, and re-layouts  6.31 us

profile of v1, /device:TPU:0, one launch (start us, length us, event | category | flops | bytes accessed | tf_op | source)
XLA Modules:
  0.0 45.5 jit_solution(4131672037245788983)
XLA Ops:
  0.6 0.0 copy-start.3
  0.6 0.7 %copy.7.recv_ref = s32[1,3,64]{2,1,0:T(4,128)S(1)} copy(s32[1,3,64]{2,0,1:T(1,128)} %param.6) | data formatting | bytes 1536 | tf_op args[1]
  1.3 0.0 copy-done.3
  1.3 0.0 copy-start
  1.3 1.2 %copy-done = f32[4,128,512]{2,1,0:T(8,128)S(1)} copy-done((f32[4,128,512]{2,1,0:T(8,128)S(1)}, f32[4,128,512]{2,1,0:T(8,128)}, u32[]{:S(2)}) %copy-start) | copy-done | bytes 1048600
  2.6 0.0 copy-start.1
  2.6 1.2 %copy-done.1 = f32[1,4,128,512]{3,2,1,0:T(8,128)S(1)} copy-done((f32[1,4,128,512]{3,2,1,0:T(8,128)S(1)}, f32[1,4,128,512]{3,2,1,0:T(8,128)}, u32[]{:S(2)}) %copy-start.1) | copy-done | bytes 1048600
  3.8 0.0 copy-start.2
  3.8 1.2 %copy-done.2 = f32[1,4,128,512]{3,2,1,0:T(8,128)S(1)} copy-done((f32[1,4,128,512]{3,2,1,0:T(8,128)S(1)}, f32[1,4,128,512]{3,2,1,0:T(8,128)}, u32[]{:S(2)}) %copy-start.2) | copy-done | bytes 1048600
  5.0 38.6 %shard_map.68 = (f32[1,4,128,512]{3,2,1,0:T(8,128)S(1)}, f32[4,128,512]{2,1,0:T(8,128)S(1)}) custom-call(f32[4,128,512]{2,1,0:T(8,128)S(1)} %copy-done, s32[1,3,64]{2,1,0:T(4,128)S(1)} %copy.7.recv_ref, f32[1,64]{1,0:T(1,128)S(1)} %copy-done.3, f32[1,4,128,512]{3,2,1,0:T(8,128)S(1)} %copy-done.1, f32[1,4,128,512]{3,2,1,0:T(8,128)S(1)} %copy-done.2), custom_call_target="tpu_custom_call" | custom-call | tf_op jit(solution)/shard_map/pallas_call | solution.py:390
  43.6 1.0 %copy.10 = f32[1,4,128,512]{3,2,1,0:T(8,128)} copy(f32[1,4,128,512]{3,2,1,0:T(8,128)S(1)} %get-tuple-element.4) | data formatting | bytes 2097152
  44.6 1.0 %copy.11 = f32[4,128,512]{2,1,0:T(8,128)} copy(f32[4,128,512]{2,1,0:T(8,128)S(1)} %get-tuple-element.5) | data formatting | bytes 2097152
Async XLA Ops:
  0.6 0.7 %copy-start.3 = (f32[1,64]{1,0:T(1,128)S(1)}, f32[1,64]{1,0:T(1,128)}, u32[]{:S(2)}) copy-start(f32[1,64]{1,0:T(1,128)} %obs_ref.1) | copy-start | bytes 772
  1.3 1.2 %copy-start = (f32[4,128,512]{2,1,0:T(8,128)S(1)}, f32[4,128,512]{2,1,0:T(8,128)}, u32[]{:S(2)}) copy-start(f32[4,128,512]{2,1,0:T(8,128)} %cond_hbm.1) | copy-start | bytes 3145732
  2.6 1.2 %copy-start.1 = (f32[1,4,128,512]{3,2,1,0:T(8,128)S(1)}, f32[1,4,128,512]{3,2,1,0:T(8,128)}, u32[]{:S(2)}) copy-start(f32[1,4,128,512]{3,2,1,0:T(8,128)} %pot_hbm.1) | copy-start | bytes 3145732
  3.8 1.2 %copy-start.2 = (f32[1,4,128,512]{3,2,1,0:T(8,128)S(1)}, f32[1,4,128,512]{3,2,1,0:T(8,128)}, u32[]{:S(2)}) copy-start(f32[1,4,128,512]{3,2,1,0:T(8,128)} %adj_hbm.1) | copy-start | bytes 3145732

commit v2 on v1

--- a/solution.py
+++ b/solution.py
@@ -10,6 +10,8 @@
 relax_weight = 0.8
 MESH = pl.DeviceIdType.MESH
 PAD = 8
+UNROLLS = (4, 2, 1)
+VMEM_LIMIT = 32 * 1024 * 1024
 CHUNKS = 4
 COND, ADJ0, POT, ADJ1, ADJ2 = range(5)
 UP, DOWN = 0, 1
@@ -19,12 +21,13 @@
 def kernel(
     counts,
     cond_hbm,
-    recv_ref,
-    obs_ref,
+    recv_hbm,
+    obs_hbm,
     pot_hbm,
     adj_hbm,
     adj_out,
-    grad_out,
+    grad,
+    grad_far,
     cond,
     adj0,
     pot,
@@ -32,10 +35,9 @@
     adj2,
     source,
     weight,
-    grad,
-    grad_far,
+    recv_ref,
+    obs_ref,
     load_sem,
-    out_sem,
     z_send,
     z_recv,
     y_send,
@@ -72,6 +74,8 @@
                 hbm_of[field], vmem_of[field].at[pl.ds(1, planes), inside], load_sem.at[field]
             )
         )
+    loads.append(pltpu.make_async_copy(recv_hbm, recv_ref, load_sem.at[3]))
+    loads.append(pltpu.make_async_copy(obs_hbm, obs_ref, load_sem.at[4]))
     for copy in loads:
         copy.start()
 
@@ -190,7 +194,7 @@
 
     for way in (UP, DOWN):
         start_z(COND, way, 0)
-    for part in range(CHUNKS):
+    for part in [0] + ([CHUNKS - 1] if CHUNKS > 1 else []) + list(range(1, CHUNKS - 1)):
         for way in (UP, DOWN):
             start_z(ADJ0, way, part)
     for field in (COND, ADJ0, POT):
@@ -200,8 +204,8 @@
         copy.wait()
 
     recv_count = recv_ref.shape[-1]
-    z_at = recv_ref[0, 0:1, :] - gz * planes
-    y_at = recv_ref[0, 1:2, :] - gy * rows
+    z_at = recv_ref[0] - gz * planes
+    y_at = recv_ref[1] - gy * rows
     near = (z_at >= 0) & (z_at < planes) & (y_at >= 0) & (y_at < rows)
     line = jnp.where(near, z_at * rows + y_at, -1)
     eye = lax.broadcasted_iota(jnp.int32, (recv_count, recv_count), 0) == lax.broadcasted_iota(
@@ -213,7 +217,7 @@
         return jnp.sum(jnp.where(eye, wide, 0.0), axis=1, keepdims=True)
 
     line_col = column(line).astype(jnp.int32)
-    x_col = column(recv_ref[0, 2:3, :]).astype(jnp.int32)
+    x_col = column(recv_ref[2]).astype(jnp.int32)
     obs_col = column(obs_ref[...])
     picked = jnp.zeros((recv_count, lanes), jnp.float32)
     along = lax.broadcasted_iota(jnp.int32, (recv_count, rows), 1)
@@ -274,7 +278,10 @@
             w = weight[plane - 1, pl.ds(pl.multiple_of(r - PAD, 8), 8)]
         s = source[plane - 1, pl.ds(pl.multiple_of(r - PAD, 8), 8)]
         coupled = 0.5 * (c * sum_a + sum_q)
-        new[plane, pl.ds(r, 8)] = (1.0 - relax_weight) * a + w * (s + coupled)
+        value = (1.0 - relax_weight) * a + w * (s + coupled)
+        new[plane, pl.ds(r, 8)] = value
+        if not first:
+            adj_out[0, plane - 1, pl.ds(pl.multiple_of(r - PAD, 8), 8)] = value
 
     def grad_block(plane, r):
         p = pot[plane, pl.ds(r, 8)]
@@ -285,19 +292,38 @@
         grad[plane - 1, pl.ds(pl.multiple_of(r - PAD, 8), 8)] = -0.5 * total
 
     def over_rows(first_row, count, action):
+        blocks = count // 8
+        step = next(n for n in UNROLLS if blocks % n == 0)
+
         def body(i, carry):
-            action(pl.multiple_of(PAD + first_row + i * 8, 8))
+            for k in range(step):
+                action(pl.multiple_of(PAD + first_row + (i * step + k) * 8, 8))
             return carry
 
-        lax.fori_loop(0, count // 8, body, 0)
+        lax.fori_loop(0, blocks // step, body, 0)
 
     inner = list(range(2, planes))
     edges = [(1, UP), (planes, DOWN)]
 
-    wait_y(COND)
-    wait_y(ADJ0)
-    for plane in inner:
-        over_rows(0, rows, lambda r: relax_block(adj0, adj1, plane, r, True))
+    parts = [0] + ([CHUNKS - 1] if CHUNKS > 1 else []) + list(range(1, CHUNKS - 1))
+    rims = [0, rows - 8]
+
+    def sweep_inner(action, field):
+        for plane in inner:
+            over_rows(8, rows - 16, lambda r: action(plane, r))
+        for each in field:
+            wait_y(each)
+        for plane in inner:
+            for r in rims:
+                action(plane, PAD + r)
+
+    def first_block(plane, r):
+        relax_block(adj0, adj1, plane, r, True)
+
+    def second_block(plane, r):
+        relax_block(adj1, adj2, plane, r, False)
+
+    sweep_inner(first_block, (COND, ADJ0))
     for way in (UP, DOWN):
 
         def pass_on():
@@ -307,57 +333,43 @@
         guarded(z_from[way], pass_on)
     for way in (UP, DOWN):
         guarded(z_from[way], lambda: relay(way).wait())
-    for part in range(CHUNKS):
+    for i, part in enumerate(parts):
         for plane, way in edges:
             wait_z(ADJ0, way, part)
-            over_rows(part * chunk, chunk, lambda r: relax_block(adj0, adj1, plane, r, True))
+            over_rows(part * chunk, chunk, lambda r: first_block(plane, r))
             start_z(ADJ1, 1 - way, part)
-    start_y(ADJ1)
-    for part in range(CHUNKS):
+        if i == min(1, CHUNKS - 1):
+            start_y(ADJ1)
+    for part in parts:
         for way in (UP, DOWN):
             start_z(POT, way, part)
 
-    wait_y(ADJ1)
-    for plane in inner:
-        over_rows(0, rows, lambda r: relax_block(adj1, adj2, plane, r, False))
-    for part in range(CHUNKS):
+    sweep_inner(second_block, (ADJ1,))
+    for i, part in enumerate(parts):
         for plane, way in edges:
             wait_z(ADJ1, way, part)
-            over_rows(part * chunk, chunk, lambda r: relax_block(adj1, adj2, plane, r, False))
+            over_rows(part * chunk, chunk, lambda r: second_block(plane, r))
             start_z(ADJ2, 1 - way, part)
-    start_y(ADJ2)
-    adj_store = pltpu.make_async_copy(
-        adj2.at[pl.ds(1, planes), inside], adj_out.at[0], out_sem.at[0]
-    )
-    adj_store.start()
-
-    wait_y(POT)
-    wait_y(ADJ2)
+        if i == min(1, CHUNKS - 1):
+            start_y(ADJ2)
+
+    sweep_inner(grad_block, (POT, ADJ2))
     sent = []
     for plane in inner:
-        over_rows(0, rows, lambda r: grad_block(plane, r))
         for part in range(CHUNKS):
             sent.append((plane - 1) * CHUNKS + part)
             g_copy(sent[-1]).start()
-    for part in range(CHUNKS):
+    for part in parts:
         for plane, way in edges:
             wait_z(POT, way, part)
             wait_z(ADJ2, way, part)
             over_rows(part * chunk, chunk, lambda r: grad_block(plane, r))
             sent.append((plane - 1) * CHUNKS + part)
             g_copy(sent[-1]).start()
-    stores = []
     for part in sent:
         plane, start = part // CHUNKS, (part % CHUNKS) * chunk
         at = pl.ds(start, chunk)
         g_copy(part).wait_recv()
-        grad_far[plane, at] = grad_far[plane, at] + grad[plane, at]
-        stores.append(
-            pltpu.make_async_copy(
-                grad_far.at[plane, at], grad_out.at[plane, at], out_sem.at[1 + part]
-            )
-        )
-        stores[-1].start()
 
     for part in sent:
         g_copy(part).wait_send()
@@ -375,31 +387,31 @@
 
         guarded(z_has[way], z_done)
         guarded(y_has[way], y_done)
-    adj_store.wait()
-    for store in stores:
-        store.wait()
 
 
 def local(counts, conductivity, receivers, observed, potential, adjoint_prev):
     planes, rows, lanes = conductivity.shape
+    receivers = jnp.transpose(receivers, (1, 0, 2))
     wide = pltpu.VMEM((planes + 2, rows + 2 * PAD, lanes), jnp.float32)
     body = pltpu.VMEM((planes, rows, lanes), jnp.float32)
     dma = pltpu.SemaphoreType.DMA
-    anywhere = pl.BlockSpec(memory_space=pl.ANY)
+    in_hbm = pl.BlockSpec(memory_space=pltpu.HBM)
     in_vmem = pl.BlockSpec(memory_space=pltpu.VMEM)
-    return pl.pallas_call(
+    adjoint, own, far = pl.pallas_call(
         functools.partial(kernel, counts),
         out_shape=(
             jax.ShapeDtypeStruct(adjoint_prev.shape, jnp.float32),
             jax.ShapeDtypeStruct(conductivity.shape, jnp.float32),
+            jax.ShapeDtypeStruct(conductivity.shape, jnp.float32),
         ),
-        in_specs=[anywhere, in_vmem, in_vmem, anywhere, anywhere],
-        out_specs=(anywhere, anywhere),
+        in_specs=[in_hbm] * 5,
+        out_specs=(in_vmem,) * 3,
         scratch_shapes=[wide] * 5
-        + [body] * 4
+        + [body] * 2
         + [
-            dma((3,)),
-            dma((1 + planes * CHUNKS,)),
+            pltpu.VMEM(receivers.shape, jnp.int32),
+            pltpu.VMEM(observed.shape, jnp.float32),
+            dma((5,)),
             dma((5, 2, CHUNKS)),
             dma((5, 2, CHUNKS)),
             dma((5, 2)),
@@ -410,9 +422,15 @@
             dma((planes * CHUNKS,)),
         ],
         compiler_params=pltpu.CompilerParams(
-            collective_id=0, has_side_effects=True, vmem_limit_bytes=40 * 1024 * 1024
+            collective_id=0, has_side_effects=True, vmem_limit_bytes=VMEM_LIMIT
         ),
-    )(conductivity, receivers, observed, potential, adjoint_prev)
+    )(
+        *(
+            pltpu.with_memory_space_constraint(x, pltpu.HBM)
+            for x in (conductivity, receivers, observed, potential, adjoint_prev)
+        )
+    )
+    return adjoint, own + far
 
 
 def solution(mesh):

time: 45.8 us -> 35.9 us (0.78)
  Pallas kernels: 38.6 us -> 33 us
  local copies, waits for them, and re-layouts: 6.31 us -> 0.97 us
  other arithmetic: 0 us -> 1.18 us
    pallas_call x1, Pallas kernels: 38.6 us -> 33 us  [local(): pl.pallas_call(functools.partial(kernel, counts), out_shape=(jax.ShapeDty...]
    unnamed x11 -> x1, local copies, waits for them, and re-layouts: 6.31 us -> 0.97 us
    add x0 -> x1, other arithmetic: none -> 1.18 us  [local(): return (adjoint, own + far)]
where the time goes in v2:
time: 35.9 us; the launch traced here: 35.7 us
  Pallas kernels  33 us (92%)
  other arithmetic  1.18 us (3%)
  local copies, waits for them, and re-layouts  0.97 us (3%)
  between operations  0.64 us (2%)
    pallas_call x1, Pallas kernels, local(): pl.pallas_call(functools.partial(kernel, counts), out_shape=(jax.ShapeDty...  33 us
    add x1, other arithmetic, local(): return (adjoint, own + far)  1.18 us
    unnamed x1, local copies, waits for them, and re-layouts  0.97 us

profile of v2, /device:TPU:0, one launch (start us, length us, event | category | flops | bytes accessed | tf_op | source)
XLA Modules:
  0.0 35.7 jit_solution(3622609211120140032)
XLA Ops:
  0.6 33.0 %shard_map.68 = (f32[1,4,128,512]{3,2,1,0:T(8,128)S(1)}, f32[4,128,512]{2,1,0:T(8,128)S(1)}, f32[4,128,512]{2,1,0:T(8,128)S(1)}) custom-call(f32[4,128,512]{2,1,0:T(8,128)} %cond_hbm.1, s32[3,1,64]{2,1,0:T(1,128)} %bitcast.1, f32[1,64]{1,0:T(1,128)} %obs_hbm.1, f32[1,4,128,512]{3,2,1,0:T(8,128)} %pot_hbm.1, f32[1,4,128,512]{3,2,1,0:T(8,128)} %adj_hbm.1), custom_call_target="tpu_custom_call" | custom-call | tf_op jit(solution)/shard_map/pallas_call | solution.py:400
  33.6 1.2 %add.3 = f32[4,128,512]{2,1,0:T(8,128)} add(f32[4,128,512]{2,1,0:T(8,128)S(1)} %get-tuple-element.6, f32[4,128,512]{2,1,0:T(8,128)S(1)} %get-tuple-element.7) | non-fusion elementwise | flops 262144 | bytes 3145728 | tf_op jit(solution)/shard_map/add | solution.py:433
  34.8 1.0 %copy.8 = f32[1,4,128,512]{3,2,1,0:T(8,128)} copy(f32[1,4,128,512]{3,2,1,0:T(8,128)S(1)} %get-tuple-element.10) | data formatting | bytes 2097152

commit v3 on v2

--- a/solution.py
+++ b/solution.py
@@ -11,9 +11,11 @@
 MESH = pl.DeviceIdType.MESH
 PAD = 8
 UNROLLS = (4, 2, 1)
+FINISH_LIMIT = 8 * 1024 * 1024
 VMEM_LIMIT = 32 * 1024 * 1024
 CHUNKS = 4
-COND, ADJ0, POT, ADJ1, ADJ2 = range(5)
+SPLIT = 4
+COND, ADJ0, POT, ADJ1, ADJ2, FACE = range(6)
 UP, DOWN = 0, 1
 HIGH = lax.Precision.HIGHEST
 
@@ -35,6 +37,7 @@
     adj2,
     source,
     weight,
+    face,
     recv_ref,
     obs_ref,
     load_sem,
@@ -64,6 +67,19 @@
     y_to = ({"gy": gy + 1}, {"gy": gy - 1})
     inside = pl.ds(PAD, rows)
 
+    parts = [0, CHUNKS - 1] + list(range(1, CHUNKS - 1))
+
+    def computes(way, part):
+        turn = parts.index(part)
+        return turn >= SPLIT or turn % 2 == way
+
+    def moves(field, way, part):
+        if field == COND:
+            return part == 0
+        if field in (POT, ADJ2):
+            return computes(way, part)
+        return field != FACE or not computes(way, part)
+
     hbm_of = {COND: cond_hbm, ADJ0: adj_hbm.at[0], POT: pot_hbm.at[0]}
     vmem_of = {COND: cond, ADJ0: adj0, POT: pot, ADJ1: adj1, ADJ2: adj2}
 
@@ -115,6 +131,16 @@
     pl.semaphore_wait(barrier, neighbours)
 
     def z_copy(field, way, part):
+        if field == FACE:
+            at = pl.ds(part * chunk, chunk)
+            return pltpu.make_async_remote_copy(
+                src_ref=face.at[1 - way, at],
+                dst_ref=face.at[way, at],
+                send_sem=z_send.at[field, way, part],
+                recv_sem=z_recv.at[field, way, part],
+                device_id=z_to[way],
+                device_id_type=MESH,
+            )
         buf = vmem_of[field]
         ghost = 0 if way == UP else top
         if field == COND:
@@ -161,14 +187,16 @@
             device_id_type=MESH,
         )
 
-    def g_copy(part):
-        plane = part // CHUNKS
-        at = pl.ds((part % CHUNKS) * chunk, chunk)
+    def g_copy(plane, part):
+        if part is None:
+            at, index = pl.ds(0, rows), 2 * CHUNKS + plane
+        else:
+            at, index = pl.ds(part * chunk, chunk), part + (CHUNKS if plane else 0)
         return pltpu.make_async_remote_copy(
             src_ref=grad.at[plane, at],
             dst_ref=grad_far.at[plane, at],
-            send_sem=g_send.at[part],
-            recv_sem=g_recv.at[part],
+            send_sem=g_send.at[index],
+            recv_sem=g_recv.at[index],
             device_id={"pat": partner},
             device_id_type=MESH,
         )
@@ -179,9 +207,13 @@
             action()
 
     def start_z(field, way, part):
+        if not moves(field, way, part):
+            return
         guarded(z_has[way], lambda: z_copy(field, way, part).start())
 
     def wait_z(field, way, part):
+        if not moves(field, way, part):
+            return
         guarded(z_from[way], lambda: z_copy(field, way, part).wait_recv())
 
     def start_y(field):
@@ -194,7 +226,7 @@
 
     for way in (UP, DOWN):
         start_z(COND, way, 0)
-    for part in [0] + ([CHUNKS - 1] if CHUNKS > 1 else []) + list(range(1, CHUNKS - 1)):
+    for part in parts:
         for way in (UP, DOWN):
             start_z(ADJ0, way, part)
     for field in (COND, ADJ0, POT):
@@ -287,9 +319,24 @@
         p = pot[plane, pl.ds(r, 8)]
         a = adj2[plane, pl.ds(r, 8)]
         total = (p - left_of(p)) * (a - left_of(a)) + (p - right_of(p)) * (a - right_of(a))
-        for p_n, a_n in zip(beside(pot, plane, r, p), beside(adj2, plane, r, a)):
+        pairs = list(zip(beside(pot, plane, r, p), beside(adj2, plane, r, a)))
+        if plane == 1:
+            del pairs[2]
+        elif plane == planes:
+            del pairs[3]
+        for p_n, a_n in pairs:
             total = total + (p - p_n) * (a - a_n)
         grad[plane - 1, pl.ds(pl.multiple_of(r - PAD, 8), 8)] = -0.5 * total
+
+    def face_block(plane, way, r):
+        ghost = 0 if way == UP else top
+        p = pot[plane, pl.ds(r, 8)] - pot[ghost, pl.ds(r, 8)]
+        a = adj2[plane, pl.ds(r, 8)] - adj2[ghost, pl.ds(r, 8)]
+        face[way, pl.ds(pl.multiple_of(r - PAD, 8), 8)] = p * a
+
+    def close_block(plane, way, r):
+        at = pl.ds(pl.multiple_of(r - PAD, 8), 8)
+        grad[plane - 1, at] = grad[plane - 1, at] - 0.5 * face[way, at]
 
     def over_rows(first_row, count, action):
         blocks = count // 8
@@ -305,7 +352,6 @@
     inner = list(range(2, planes))
     edges = [(1, UP), (planes, DOWN)]
 
-    parts = [0] + ([CHUNKS - 1] if CHUNKS > 1 else []) + list(range(1, CHUNKS - 1))
     rims = [0, rows - 8]
 
     def sweep_inner(action, field):
@@ -353,33 +399,53 @@
         if i == min(1, CHUNKS - 1):
             start_y(ADJ2)
 
-    sweep_inner(grad_block, (POT, ADJ2))
+    for plane in inner:
+        over_rows(8, rows - 16, lambda r: grad_block(plane, r))
+    for plane, way in edges:
+        over_rows(8, rows - 16, lambda r: grad_block(plane, r))
+    wait_y(POT)
+    wait_y(ADJ2)
+    for plane in inner + [1, planes]:
+        for r in rims:
+            grad_block(plane, PAD + r)
     sent = []
+
+    def send_grad(plane, part):
+        sent.append((plane, part))
+        g_copy(plane, part).start()
+
     for plane in inner:
-        for part in range(CHUNKS):
-            sent.append((plane - 1) * CHUNKS + part)
-            g_copy(sent[-1]).start()
+        send_grad(plane - 1, None)
     for part in parts:
         for plane, way in edges:
-            wait_z(POT, way, part)
-            wait_z(ADJ2, way, part)
-            over_rows(part * chunk, chunk, lambda r: grad_block(plane, r))
-            sent.append((plane - 1) * CHUNKS + part)
-            g_copy(sent[-1]).start()
-    for part in sent:
-        plane, start = part // CHUNKS, (part % CHUNKS) * chunk
-        at = pl.ds(start, chunk)
-        g_copy(part).wait_recv()
-
-    for part in sent:
-        g_copy(part).wait_send()
+
+            def make_face():
+                over_rows(part * chunk, chunk, lambda r: face_block(plane, way, r))
+
+            if computes(way, part):
+                wait_z(POT, way, part)
+                wait_z(ADJ2, way, part)
+                make_face()
+                start_z(FACE, 1 - way, part)
+            else:
+                guarded(jnp.logical_not(z_from[way]), make_face)
+    for part in parts[SPLIT:] + parts[:SPLIT]:
+        for plane, way in edges:
+            wait_z(FACE, way, part)
+            over_rows(part * chunk, chunk, lambda r: close_block(plane, way, r))
+            send_grad(plane - 1, part)
+    for plane, part in sent:
+        g_copy(plane, part).wait_recv()
+    for plane, part in sent:
+        g_copy(plane, part).wait_send()
     for way in (UP, DOWN):
 
         def z_done():
             z_copy(COND, way, 0).wait_send()
-            for field in (ADJ0, POT, ADJ1, ADJ2):
+            for field in (ADJ0, POT, ADJ1, ADJ2, FACE):
                 for part in range(CHUNKS):
-                    z_copy(field, way, part).wait_send()
+                    if moves(field, way, part):
+                        z_copy(field, way, part).wait_send()
 
         def y_done():
             for field in range(5):
@@ -387,6 +453,18 @@
 
         guarded(z_has[way], z_done)
         guarded(y_has[way], y_done)
+
+
+def finish(adjoint, own, far, adj_out, grad_out, total, sems):
+    planes = own.shape[0]
+    copies = [pltpu.make_async_copy(adjoint, adj_out, sems.at[planes])]
+    copies[0].start()
+    for plane in range(planes):
+        total[plane] = own[plane] + far[plane]
+        copies.append(pltpu.make_async_copy(total.at[plane], grad_out.at[plane], sems.at[plane]))
+        copies[-1].start()
+    for copy in copies:
+        copy.wait()
 
 
 def local(counts, conductivity, receivers, observed, potential, adjoint_prev):
@@ -408,18 +486,19 @@
         out_specs=(in_vmem,) * 3,
         scratch_shapes=[wide] * 5
         + [body] * 2
+        + [pltpu.VMEM((2, rows, lanes), jnp.float32)]
         + [
             pltpu.VMEM(receivers.shape, jnp.int32),
             pltpu.VMEM(observed.shape, jnp.float32),
             dma((5,)),
-            dma((5, 2, CHUNKS)),
-            dma((5, 2, CHUNKS)),
+            dma((6, 2, CHUNKS)),
+            dma((6, 2, CHUNKS)),
             dma((5, 2)),
             dma((5, 2)),
             dma((2,)),
             dma((2,)),
-            dma((planes * CHUNKS,)),
-            dma((planes * CHUNKS,)),
+            dma((2 * CHUNKS + planes,)),
+            dma((2 * CHUNKS + planes,)),
         ],
         compiler_params=pltpu.CompilerParams(
             collective_id=0, has_side_effects=True, vmem_limit_bytes=VMEM_LIMIT
@@ -430,7 +509,18 @@
             for x in (conductivity, receivers, observed, potential, adjoint_prev)
         )
     )
-    return adjoint, own + far
+    anywhere = pl.BlockSpec(memory_space=pl.ANY)
+    return pl.pallas_call(
+        finish,
+        out_shape=(
+            jax.ShapeDtypeStruct(adjoint.shape, jnp.float32),
+            jax.ShapeDtypeStruct(own.shape, jnp.float32),
+        ),
+        in_specs=[in_vmem] * 3,
+        out_specs=(anywhere, anywhere),
+        scratch_shapes=[body, dma((planes + 1,))],
+        compiler_params=pltpu.CompilerParams(vmem_limit_bytes=FINISH_LIMIT),
+    )(adjoint, own, far)
 
 
 def solution(mesh):

time: 35.9 us -> 32.8 us (0.914)
  other arithmetic: 1.18 us -> 0 us
  Pallas kernels: 33 us -> 32 us
  local copies, waits for them, and re-layouts: 0.97 us -> 0 us
    pallas_call x1, Pallas kernels: 33 us -> 30.6 us  [local(): pl.pallas_call(functools.partial(kernel, counts), out_shape=(jax.ShapeDty...]
    pallas_call x0 -> x1, Pallas kernels: none -> 1.35 us  [local(): pl.pallas_call(finish, out_shape=(jax.ShapeDtypeStruct(adjoint.shape, jnp...]
    add x1 -> x0, other arithmetic: 1.18 us -> none  [local(): return (adjoint, own + far)]
    unnamed x1 -> x0, local copies, waits for them, and re-layouts: 0.97 us -> none
where the time goes in v3:
time: 32.8 us; the launch traced here: 32.6 us
  Pallas kernels  32 us (98%)
  between operations  0.64 us (2%)
    pallas_call x1, Pallas kernels, local(): pl.pallas_call(functools.partial(kernel, counts), out_shape=(jax.ShapeDty...  30.6 us
    pallas_call x1, Pallas kernels, local(): pl.pallas_call(finish, out_shape=(jax.ShapeDtypeStruct(adjoint.shape, jnp...  1.35 us

profile of v3, /device:TPU:0, one launch (start us, length us, event | category | flops | bytes accessed | tf_op | source)
XLA Modules:
  0.0 32.6 jit_solution(11659794563383291560)
XLA Ops:
  0.6 30.6 %shard_map.68 = (f32[1,4,128,512]{3,2,1,0:T(8,128)S(1)}, f32[4,128,512]{2,1,0:T(8,128)S(1)}, f32[4,128,512]{2,1,0:T(8,128)S(1)}) custom-call(f32[4,128,512]{2,1,0:T(8,128)} %cond_hbm.1, s32[3,1,64]{2,1,0:T(1,128)} %bitcast.1, f32[1,64]{1,0:T(1,128)} %obs_hbm.1, f32[1,4,128,512]{3,2,1,0:T(8,128)} %pot_hbm.1, f32[1,4,128,512]{3,2,1,0:T(8,128)} %adj_hbm.1), custom_call_target="tpu_custom_call" | custom-call | tf_op jit(solution)/shard_map/pallas_call | solution.py:478
  31.3 1.4 %shard_map.69 = (f32[1,4,128,512]{3,2,1,0:T(8,128)}, f32[4,128,512]{2,1,0:T(8,128)}) custom-call(f32[1,4,128,512]{3,2,1,0:T(8,128)S(1)} %get-tuple-element.5.adjoint, f32[4,128,512]{2,1,0:T(8,128)S(1)} %get-tuple-element.6.own, f32[4,128,512]{2,1,0:T(8,128)S(1)} %get-tuple-element.7.far), custom_call_target="tpu_custom_call" | custom-call | tf_op jit(solution)/shard_map/pallas_call | solution.py:513
